TPU v7x, 32 devices: a whole 2x2x4 slice. The times are simulated.
32 devices in a mesh: seq: 16 (over z, x, core), head: 2 (over y).
Axes of the slice: x: 2, y: 2, z: 4, core: 2. Of those that a mesh axis runs over, the one named last changes fastest.
Arguments:
- fw_query: bfloat16 [6144, 4096], P('seq', 'head'), may hold values from -6 to 6
- fw_key: bfloat16 [6144, 4096], P('seq', 'head'), may hold values from -6 to 6
- fw_value: bfloat16 [6144, 4096], P('seq', 'head'), may hold values from -6 to 6
- learn_rate: float32 [6144, 8], P('seq', 'head'), may hold values from 0.00025515517 to 0.002551552
- fast_weights: bfloat16 [3, 8, 512, 512], P(None, 'head'), may hold values from -0.25 to 0.25
- attn_query: bfloat16 [6144, 4096], P(('seq', 'head')), may hold values from -32 to 32
- attn_key: bfloat16 [6144, 1024], P(('seq', 'head')), may hold values from -32 to 32
- attn_value: bfloat16 [6144, 1024], P(('seq', 'head')), may hold values from -6 to 6
Outputs:
- mixed: bfloat16 [6144, 4096], P(('seq', 'head'))
All inputs are finite; a program needn't handle non-finite values.
Results may differ from a plain program's by a relative error of at most 0.01.
Values may be sent and summed in bfloat16 or wider, within the bound.
A program may use at most 128 MiB of HBM per device.

v0:
```python
import functools
import math

import jax
import jax.numpy as jnp
from jax import lax
from jax.experimental import pallas as pl
from jax.experimental.pallas import tpu as pltpu
from jax.sharding import PartitionSpec as P

Q_HEADS = 32
KV_HEADS = 8
HEAD_DIM = 128
WINDOW = 256


def shifted(value, axis, by):
    devices = lax.axis_size(axis)
    pairs = [(i, i + by) for i in range(devices) if 0 <= i + by < devices]
    return lax.ppermute(value, axis, pairs)


def local_grads(keys, values, rates, weights):
    pre_gate = jnp.einsum("thd,hde->the", keys, weights[0], preferred_element_type=jnp.float32)
    pre_up = jnp.einsum("thd,hde->the", keys, weights[1], preferred_element_type=jnp.float32)
    sigm = jax.nn.sigmoid(pre_gate)
    hidden = (pre_gate * sigm * pre_up).astype(jnp.bfloat16)
    scaled = (rates[:, :, None] * values.astype(jnp.float32)).astype(jnp.bfloat16)
    back = jnp.einsum("the,hde->thd", scaled, weights[2], preferred_element_type=jnp.float32)
    d_gate = (back * pre_up * sigm * (1.0 + pre_gate * (1.0 - sigm))).astype(jnp.bfloat16)
    d_up = (back * pre_gate * sigm).astype(jnp.bfloat16)
    grad_gate = jnp.einsum("thd,the->hde", keys, d_gate, preferred_element_type=jnp.float32)
    grad_up = jnp.einsum("thd,the->hde", keys, d_up, preferred_element_type=jnp.float32)
    grad_down = jnp.einsum("thd,the->hde", hidden, scaled, preferred_element_type=jnp.float32)
    return jnp.stack([grad_gate, grad_up, grad_down])


def renorm(summed, start_weights):
    start = start_weights.astype(jnp.float32)
    stepped = start + summed
    ratio = jnp.sqrt(jnp.mean(start * start, axis=-2, keepdims=True)) * lax.rsqrt(
        jnp.mean(stepped * stepped, axis=-2, keepdims=True) + 1e-06
    )
    return (stepped * ratio).astype(jnp.bfloat16)


def on_device(
    fw_query, fw_key, fw_value, learn_rate, fast_weights, attn_query, attn_key, attn_value
):
    tok_rows = fw_key.shape[0]
    local_heads = fast_weights.shape[1]
    width = fast_weights.shape[2]
    keys = fw_key.reshape(tok_rows, local_heads, width)
    values = fw_value.reshape(tok_rows, local_heads, width)
    queries = fw_query.reshape(tok_rows, local_heads, width)
    grads = local_grads(keys, values, learn_rate, fast_weights)
    share = lax.psum_scatter(grads, "seq", scatter_dimension=3, tiled=True)
    columns = share.shape[3]
    start_cols = lax.dynamic_slice_in_dim(fast_weights, lax.axis_index("seq") * columns, columns, 3)
    fresh_part = renorm(share, start_cols)
    fresh = lax.all_gather(fresh_part, "seq", axis=3, tiled=True)
    q_gate = jnp.einsum("thd,hde->the", queries, fresh[0], preferred_element_type=jnp.float32)
    q_up = jnp.einsum("thd,hde->the", queries, fresh[1], preferred_element_type=jnp.float32)
    answer_hidden = (q_gate * jax.nn.sigmoid(q_gate) * q_up).astype(jnp.bfloat16)
    fw_out = jnp.einsum(
        "the,hef->thf", answer_hidden, fresh[2], preferred_element_type=jnp.float32
    ).astype(jnp.bfloat16)
    fw_out = fw_out.reshape(tok_rows, local_heads * width)
    fw_fine = lax.all_to_all(fw_out, "head", split_axis=0, concat_axis=1, tiled=True)
    rows = attn_query.shape[0]
    reach = -(-WINDOW // rows)
    kv_width = attn_key.shape[1]
    group = Q_HEADS // KV_HEADS
    buffer_k = jnp.zeros(((reach + 1) * rows, kv_width), jnp.bfloat16)
    buffer_v = jnp.zeros(((reach + 1) * rows, kv_width), jnp.bfloat16)
    buffer_k = lax.dynamic_update_slice_in_dim(buffer_k, attn_key, reach * rows, 0)
    buffer_v = lax.dynamic_update_slice_in_dim(buffer_v, attn_value, reach * rows, 0)

    def bring(step, carry):
        piece_k, piece_v, store_k, store_v = carry
        piece_k, piece_v = shifted((piece_k, piece_v), ("seq", "head"), 1)
        slot = (reach - 1 - step) * rows
        store_k = lax.dynamic_update_slice_in_dim(store_k, piece_k, slot, 0)
        store_v = lax.dynamic_update_slice_in_dim(store_v, piece_v, slot, 0)
        return (piece_k, piece_v, store_k, store_v)

    carried = lax.fori_loop(0, reach, bring, (attn_key, attn_value, buffer_k, buffer_v))
    buffer_k = carried[2].reshape((reach + 1) * rows, KV_HEADS, HEAD_DIM)
    buffer_v = carried[3].reshape((reach + 1) * rows, KV_HEADS, HEAD_DIM)
    device_pos = lax.axis_index("seq") * lax.axis_size("head") + lax.axis_index("head")
    t_pos = device_pos * rows + jnp.arange(rows, dtype=jnp.int32)
    s_pos = (device_pos - reach) * rows + jnp.arange((reach + 1) * rows, dtype=jnp.int32)
    gap = t_pos[:, None] - s_pos[None, :]
    keep = (gap >= 0) & (gap < WINDOW) & (s_pos[None, :] >= 0)
    query_heads = attn_query.reshape(rows, KV_HEADS, group, HEAD_DIM)
    scaling = 1.0 / math.sqrt(HEAD_DIM)
    scores = (
        jnp.einsum("fcgd,lcd->cgfl", query_heads, buffer_k, preferred_element_type=jnp.float32)
        * scaling
    )
    scores = jnp.where(keep, scores, -1e30)
    top = jnp.max(scores, axis=-1, keepdims=True)
    expo = jnp.exp(scores - top)
    probs = (expo / jnp.sum(expo, axis=-1, keepdims=True)).astype(jnp.bfloat16)
    attn_out = jnp.einsum("cgfl,lcd->fcgd", probs, buffer_v, preferred_element_type=jnp.float32)
    attn_out = attn_out.reshape(rows, Q_HEADS * HEAD_DIM)
    return (attn_out + fw_fine.astype(jnp.float32)).astype(jnp.bfloat16)

MESH = pl.DeviceIdType.MESH
LANES = 128
SPLIT = 1
LAG_A = 2
ROOT_B = 5
ROOT_A = 5
FIRST_ATT = 4
PREPARE = 2
DIRECT = 4
RELAY_AT = 1


def piece(p):
    return p // 3, p % 3


def fused_kernel(
    heads, width, rows,
    q_hbm, k_hbm, v_hbm, rate_hbm, w_hbm, aq_hbm, ak_hbm, av_hbm, out_ref,
    qb, kb, vb, wb, aqb, akb, avb, g, r0, rxa, rza, rxb, rzb, nw, att, bias, hidb, fsend, frecv, rate_ref, rates, via,
    in_sem, misc_sem, halo_s, halo_r, s0_s, s0_r, xa_s, xa_r, za_s, za_r, xb_s, xb_r, zb_s, zb_r,
    gax_s, gax_r, gaz_s, gaz_r, gbx_s, gbx_r, gbz_s, gbz_r, c_s, c_r, y_s, y_r, via_s, via_r, on_s,
):
    me = lax.axis_index("seq")
    y = lax.axis_index("head")
    n_seq, n_head = lax.axis_size("seq"), lax.axis_size("head")
    core, xx, z = me % 2, (me // 2) % 2, me // 4
    top = n_seq // 4 - 1
    place = z + core * (top - 2 * z)
    cb = core * 2 + xx
    ob = core * 2 + 1 - xx
    other_core = me + 1 - 2 * core
    other_x = me + 2 - 4 * xx
    ahead = me + 4 - 8 * core
    behind = me - 4 + 8 * core
    pos = me * n_head + y
    last = n_seq * n_head
    extra = WINDOW - rows
    pad = akb.shape[0] - WINDOW - rows
    half = 2 * LANES
    pairs = heads // 2
    pieces = pairs * 3
    is_root = place == top

    def cols(block, size=LANES):
        return pl.ds(pl.multiple_of(block * size, size), size)

    def remote(src, dst, ssem, rsem, seq, head=None):
        return pltpu.make_async_remote_copy(
            src_ref=src, dst_ref=dst, send_sem=ssem, recv_sem=rsem,
            device_id={"seq": seq, "head": y if head is None else head},
            device_id_type=MESH,
        )

    def loads(h):
        c = cols(h, width)
        return (
            pltpu.make_async_copy(k_hbm.at[:, c], kb.at[:, c], in_sem.at[h, 0]),
            pltpu.make_async_copy(v_hbm.at[:, c], vb.at[:, c], in_sem.at[h, 1]),
            pltpu.make_async_copy(w_hbm.at[:, h], wb.at[:, h], in_sem.at[h, 2]),
        )

    own_at = pl.ds(pad + WINDOW, rows)
    others = (
        pltpu.make_async_copy(aq_hbm, aqb, misc_sem.at[0]),
        pltpu.make_async_copy(ak_hbm, akb.at[own_at], misc_sem.at[1]),
        pltpu.make_async_copy(av_hbm, avb.at[own_at], misc_sem.at[2]),
        pltpu.make_async_copy(q_hbm, qb, misc_sem.at[3]),
    )
    rate_load = pltpu.make_async_copy(rate_hbm, rate_ref, misc_sem.at[4])
    rate_load.start()
    for i in range(heads):
        for copy in loads(i + 1 - 2 * (i % 2)):
            copy.start()
    for copy in others:
        copy.start()

    barrier = pltpu.get_barrier_semaphore()

    def greet(seq, head):
        pl.semaphore_signal(barrier, inc=1, device_id={"seq": seq, "head": head}, device_id_type=MESH)

    for seq in (other_core, other_x):
        greet(seq, y)
    greet(me, 1 - y)
    below = jnp.where(z > 0, 1, 0)
    above = jnp.where(z < top, 1, 0)

    @pl.when(z > 0)
    def _():
        greet(me - 4, y)

    @pl.when(z < top)
    def _():
        greet(me + 4, y)

    met = 3 + below + above
    for step in (1, 2):
        met = met + jnp.where(pos >= step, 1, 0) + jnp.where(pos + step < last, 1, 0)

        @pl.when(pos + step < last)
        def _():
            greet((pos + step) // n_head, (pos + step) % n_head)

        @pl.when(pos >= step)
        def _():
            greet((pos - step) // n_head, (pos - step) % n_head)

    def halo(step, c):
        there = pos + step
        seq, head = there // n_head, there % n_head
        if step == 1:
            src, dst = pl.ds(0, rows), pl.ds(pad + extra, rows)
        else:
            src, dst = pl.ds(rows - extra, extra), pl.ds(pad, extra)
        j = (step - 1) * 2
        return (
            remote(ak_hbm.at[src, cols(c)], akb.at[dst, cols(c)], halo_s.at[j, c], halo_r.at[j, c], seq, head),
            remote(av_hbm.at[src, cols(c)], avb.at[dst, cols(c)], halo_s.at[j + 1, c], halo_r.at[j + 1, c], seq, head),
        )

    across = core * y
    late = KV_HEADS - DIRECT
    late_cols = pl.ds(DIRECT * LANES, late * LANES)

    def spare(k):
        hbm = (ak_hbm, av_hbm)[k]
        return remote(hbm.at[:, late_cols], via.at[k], via_s.at[k], via_r.at[k], me, 1 - y)

    def onward(k, i):
        ref = (akb, avb)[k]
        at = cols(DIRECT + i)
        return remote(
            via.at[k, :, cols(i)], ref.at[pl.ds(pad + extra, rows), at],
            on_s.at[k, i], halo_r.at[k, DIRECT + i], (pos + 2) // n_head, (pos + 2) % n_head,
        )

    is_source = (across == 1) & (pos + 1 < last)
    is_relay = (core == 1) & (y == 0) & (pos + 2 < last)

    def halo_here(step, c):
        if step == 2:
            return pos + 2 < last
        return (pos + 1 < last) & ((c < DIRECT) | (across == 0))

    def halo_start(c, _):
        @pl.when(halo_here(1, c))
        def _():
            for copy in halo(1, c):
                copy.start()

        return 0

    def halo_start_far(c, _):
        @pl.when(halo_here(2, c))
        def _():
            for copy in halo(2, c):
                copy.start()

        return 0

    def relay_start():
        @pl.when(is_source)
        def _():
            for k in range(2):
                spare(k).start()

    def relay_on():
        @pl.when(is_relay)
        def _():
            for k in range(2):
                spare(k).wait_recv()
            for i in range(late):
                for k in range(2):
                    onward(k, i).start()

    depth = width // SPLIT
    bands = range(SPLIT)

    def band(q):
        return pl.ds(q * depth, depth)

    def f32(value):
        return value.astype(jnp.float32)

    def s0(h, m):
        return remote(g.at[h, m, :, cols(1 - core, half)], r0.at[h, m], s0_s.at[h, m], s0_r.at[h, m], other_core)

    def xa(p, q):
        hs, m = piece(p)
        return remote(
            g.at[2 * hs, m, band(q), cols(ob)], rxa.at[p, band(q)], xa_s.at[p, q], xa_r.at[p, q], other_x
        )

    def za(p, q):
        hs, m = piece(p)
        return remote(
            g.at[2 * hs, m, band(q), cols(cb)], rza.at[p, band(q)], za_s.at[p, q], za_r.at[p, q], ahead
        )

    def xb(p, q):
        hs, m = piece(p)
        return remote(
            g.at[2 * hs + 1, m, band(q), cols(ob)], rxb.at[p, band(q)], xb_s.at[p, q], xb_r.at[p, q], other_x
        )

    def zb(p, j, q):
        hs, m = piece(p)
        return remote(
            g.at[2 * hs + 1, m, band(q), cols(core * 2 + j)], rzb.at[p, j, band(q)],
            zb_s.at[p, j, q], zb_r.at[p, j, q], ahead,
        )

    def fresh(h, m, block, q):
        return nw.at[h, m, band(q), cols(block)]

    def gax(p, block, q):
        hs, m = piece(p)
        ref = fresh(2 * hs, m, block, q)
        return remote(ref, ref, gax_s.at[p, q], gax_r.at[p, q], other_x)

    def gaz(p, q):
        hs, m = piece(p)
        ref = fresh(2 * hs, m, cb, q)
        return remote(ref, ref, gaz_s.at[p, q], gaz_r.at[p, q], behind)

    def gbx(p, block, q):
        hs, m = piece(p)
        ref = fresh(2 * hs + 1, m, block, q)
        return remote(ref, ref, gbx_s.at[p, q], gbx_r.at[p, q], other_x)

    def gbz(p, j, q):
        hs, m = piece(p)
        ref = fresh(2 * hs + 1, m, core * 2 + j, q)
        return remote(ref, ref, gbz_s.at[p, j, q], gbz_r.at[p, j, q], behind)

    def pair(h, m, j, q):
        ref = fresh(h, m, core * 2 + j, q)
        return remote(ref, ref, c_s.at[h, m, j, q], c_r.at[h, m, j, q], other_core)

    def pair_from(h, m, j, q):
        ref = fresh(h, m, (1 - core) * 2 + j, q)
        return remote(ref, ref, c_s.at[h, m, j, q], c_r.at[h, m, j, q], other_core)

    def compute(h, send=True):
        for copy in loads(h):
            copy.wait()
        c = cols(h, width)
        keys = kb[:, c]
        rate = rates[h][:, :1]
        scaled = (rate * f32(vb[:, c])).astype(jnp.bfloat16)
        pre_gate = jnp.dot(keys, wb[0, h], preferred_element_type=jnp.float32)
        pre_up = jnp.dot(keys, wb[1, h], preferred_element_type=jnp.float32)
        back = lax.dot_general(
            scaled, wb[2, h], (((1,), (1,)), ((), ())), preferred_element_type=jnp.float32
        )
        sigm = jax.nn.sigmoid(pre_gate)
        tn = (((0,), (0,)), ((), ()))

        def put(m, left, right):
            g[h, m] = lax.dot_general(left, right, tn, preferred_element_type=jnp.float32).astype(g.dtype)
            if send:
                s0(h, m).start()

        d_gate = (back * pre_up * sigm * (1.0 + pre_gate * (1.0 - sigm))).astype(jnp.bfloat16)
        put(0, keys, d_gate)
        d_up = (back * pre_gate * sigm).astype(jnp.bfloat16)
        put(1, keys, d_up)
        hidden = (pre_gate * sigm * pre_up).astype(jnp.bfloat16)
        put(2, hidden, scaled)

    def own(h, m, block, part, q):
        return f32(g[h, m, band(q), cols(block)]) + f32(r0[h, m, band(q), cols(part)])

    def keep_sum(h, m, block, q, value):
        g[h, m, band(q), cols(block)] = value.astype(g.dtype)

    def finish(h, m, total):
        start = f32(wb[m, h, :, cols(cb)])
        stepped = start + total
        ratio = jnp.sqrt(jnp.mean(start * start, axis=0, keepdims=True)) * lax.rsqrt(
            jnp.mean(stepped * stepped, axis=0, keepdims=True) + 1e-06
        )
        nw[h, m, :, cols(cb)] = (stepped * ratio).astype(nw.dtype)

    def own_whole(h, m):
        return f32(g[h, m, :, cols(cb)]) + f32(r0[h, m, :, cols(xx)])

    def stage_in(p):
        hs, m = piece(p)
        h = 2 * hs
        s0(h + 1, m).wait_recv()

        @pl.when(place == 0)
        def _():
            for j in range(2):
                for q in bands:
                    keep_sum(h + 1, m, core * 2 + j, q, own(h + 1, m, core * 2 + j, j, q))
                    zb(p, j, q).start()

        s0(h, m).wait_recv()
        for q in bands:
            keep_sum(h, m, ob, q, own(h, m, ob, 1 - xx, q))
            xa(p, q).start()

    def stage_b(p):
        hs, m = piece(p)
        h = 2 * hs + 1

        @pl.when(place < top)
        def _():
            for j in range(2):
                for q in bands:
                    zb(p, j, q).wait_recv()
                    keep_sum(h, m, core * 2 + j, q, own(h, m, core * 2 + j, j, q) + f32(rzb[p, j, band(q)]))
                    zb(p, j, q).start()

        @pl.when(is_root)
        def _():
            for q in bands:
                zb(p, 1 - xx, q).wait_recv()
                keep_sum(h, m, ob, q, own(h, m, ob, 1 - xx, q) + f32(rzb[p, 1 - xx, band(q)]))
                xb(p, q).start()
            for q in bands:
                zb(p, xx, q).wait_recv()

    def stage_a(p):
        hs, m = piece(p)
        h = 2 * hs

        @pl.when(place == 0)
        def _():
            for q in bands:
                xa(p, q).wait_recv()
                keep_sum(h, m, cb, q, own(h, m, cb, xx, q) + f32(rxa[p, band(q)]))
                za(p, q).start()

        @pl.when((place > 0) & (place < top))
        def _():
            for q in bands:
                xa(p, q).wait_recv()
                za(p, q).wait_recv()
                keep_sum(h, m, cb, q, own(h, m, cb, xx, q) + f32(rxa[p, band(q)]) + f32(rza[p, band(q)]))
                za(p, q).start()

        @pl.when(is_root)
        def _():
            for q in bands:
                xa(p, q).wait_recv()
                za(p, q).wait_recv()

    def stage_root_a(p):
        hs, m = piece(p)
        h = 2 * hs
        finish(h, m, own_whole(h, m) + f32(rxa[p]) + f32(rza[p]))
        for q in bands:
            gaz(p, q).start()
            gax(p, cb, q).start()
            pair(h, m, xx, q).start()

    def stage_root_b(p):
        hs, m = piece(p)
        h = 2 * hs + 1
        for q in bands:
            xb(p, q).wait_recv()
        finish(h, m, own_whole(h, m) + f32(rzb[p, xx]) + f32(rxb[p]))
        for q in bands:
            gbx(p, cb, q).start()
            gbz(p, xx, q).start()
            pair(h, m, xx, q).start()

    def stage_down_a(p):
        hs, m = piece(p)
        for q in bands:
            gaz(p, q).wait_recv()

            @pl.when(place > 0)
            def _():
                gaz(p, q).start()

            gax(p, cb, q).start()
            pair(2 * hs, m, xx, q).start()

    def stage_down_b(p):
        hs, m = piece(p)
        for q in bands:
            gbz(p, xx, q).wait_recv()

            @pl.when(place > 0)
            def _():
                gbz(p, xx, q).start()

            pair(2 * hs + 1, m, xx, q).start()

    def stage_last_b(p):
        hs, m = piece(p)
        for q in bands:
            @pl.when(is_root)
            def _():
                gbx(p, ob, q).wait_recv()
                gbz(p, 1 - xx, q).start()

            @pl.when(place < top)
            def _():
                gbz(p, 1 - xx, q).wait_recv()

                @pl.when(place > 0)
                def _():
                    gbz(p, 1 - xx, q).start()

            pair(2 * hs + 1, m, 1 - xx, q).start()

    def stage_last_a(p):
        hs, m = piece(p)
        for q in bands:
            gax(p, ob, q).wait_recv()
            pair(2 * hs, m, 1 - xx, q).start()

    group = Q_HEADS // KV_HEADS
    scaling = 1.0 / math.sqrt(HEAD_DIM)

    def attend(c):
        for step in (1, 2):
            @pl.when(pos >= step)
            def _():
                for copy in halo(step, c):
                    copy.wait_recv()

        keys = akb[:, cols(c)]
        vals = avb[:, cols(c)]
        for j in range(group):
            qc = cols(c * group + j)
            scores = lax.dot_general(
                aqb[:, qc], keys, (((1,), (1,)), ((), ())), preferred_element_type=jnp.float32
            ) * scaling
            scores = jnp.where(bias[...] > 0.0, scores, -1e30)
            peak = jnp.max(scores, axis=-1, keepdims=True)
            expo = jnp.exp(scores - peak)
            probs = (expo / jnp.sum(expo, axis=-1, keepdims=True)).astype(jnp.bfloat16)
            att[:, qc] = jnp.dot(probs, vals, preferred_element_type=jnp.float32)

    def answer_send(h, block):
        return remote(
            fsend.at[h, :, cols(block)], frecv.at[h, :, cols(block)], y_s.at[h, block], y_r.at[h, block], me, 1 - y
        )

    def mix(value, group_of, h, block):
        at = cols((group_of * heads + h) * 4 + block)
        out_ref[:, at] = (att[:, at] + f32(value)).astype(out_ref.dtype)

    def landed(h, m, j):
        for q in bands:
            pair_from(h, m, j, q).wait_recv()

    def answer_hidden(h):
        for m in range(2):
            for j in range(2):
                landed(h, m, j)
        queries = qb[:, cols(h, width)]
        q_gate = jnp.dot(queries, nw[h, 0], preferred_element_type=jnp.float32)
        q_up = jnp.dot(queries, nw[h, 1], preferred_element_type=jnp.float32)
        hidb[h] = (q_gate * jax.nn.sigmoid(q_gate) * q_up).astype(jnp.bfloat16)

    near_half = place // 2
    early = core * near_half + (1 - core) * (1 - near_half)

    def answer(h, i):
        side = early + (i // 2) * (1 - 2 * early)
        j = xx + (i % 2) * (1 - 2 * xx)
        block = side * 2 + j

        @pl.when(side != core)
        def _():
            landed(h, 2, j)

        part = jnp.dot(hidb[h], nw[h, 2, :, cols(block)], preferred_element_type=jnp.float32).astype(jnp.bfloat16)
        low, high = f32(part[:rows]), f32(part[rows:])
        lower = jnp.zeros((rows, LANES), jnp.int32) + y < 1
        fsend[h, :, cols(block)] = jnp.where(lower, high, low).astype(jnp.bfloat16)
        answer_send(h, block).start()
        mix(jnp.where(lower, low, high), y, h, block)

    def during(p, stage):
        @pl.when((p >= 0) & (p < pieces))
        def _():
            stage(p)

    rate_load.wait()
    for h in range(heads):
        rates[h] = jnp.broadcast_to(rate_ref[h : h + 1, :], (LANES, rate_ref.shape[1])).T
    compute(1, send=False)
    pl.semaphore_wait(barrier, met)
    for m in range(3):
        s0(1, m).start()
    relay_start()
    lax.fori_loop(0, KV_HEADS, halo_start, 0)
    lax.fori_loop(0, KV_HEADS, halo_start_far, 0)
    compute(0)

    def prepare():
        for step in (1, 2):
            @pl.when(pos < step)
            def _():
                at = pl.ds(pad + extra, rows) if step == 1 else pl.ds(pad, extra)
                akb[at, :] = jnp.zeros((at.size, akb.shape[1]), akb.dtype)
                avb[at, :] = jnp.zeros((at.size, avb.shape[1]), avb.dtype)

        akb[pl.ds(0, pad), :] = jnp.zeros((pad, akb.shape[1]), akb.dtype)
        avb[pl.ds(0, pad), :] = jnp.zeros((pad, avb.shape[1]), avb.dtype)
        t_idx = lax.broadcasted_iota(jnp.int32, bias.shape, 0)
        s_idx = lax.broadcasted_iota(jnp.int32, bias.shape, 1) - (pad + WINDOW)
        gap = t_idx - s_idx
        keep = (gap >= 0) & (gap < WINDOW) & (s_idx + pos * rows >= 0)
        bias[...] = keep.astype(jnp.float32)
        for copy in others:
            copy.wait()

    done = 2 + max(ROOT_A, ROOT_B) + top + 2
    ticks = pieces + max(ROOT_A, ROOT_B) + (n_seq // 4 - 1) + 1

    def tick(t, _):
        during(t, stage_in)

        @pl.when(t < heads - 2)
        def _():
            compute(heads - 1 - t)

        @pl.when(t == RELAY_AT)
        def _():
            relay_on()

        @pl.when(place > 0)
        def _():
            during(t - place, stage_b)

        during(t - LAG_A - place, stage_a)

        @pl.when(is_root)
        def _():
            during(t - ROOT_B, stage_root_b)
            during(t - ROOT_A, stage_root_a)

        @pl.when(place < top)
        def _():
            during(t - ROOT_A - top + place, stage_down_a)
            during(t - ROOT_B - top + place, stage_down_b)

        during(t - ROOT_B - 1 - top + place, stage_last_b)
        during(t - ROOT_A - 1 - top + place, stage_last_a)

        @pl.when(t == PREPARE)
        def _():
            prepare()

        @pl.when((t >= FIRST_ATT) & (t < FIRST_ATT + KV_HEADS))
        def _():
            attend(t - FIRST_ATT)

        @pl.when((t >= done) & (t < done + 2))
        def _():
            h = t - done
            answer_hidden(h)

            def one(i, _):
                answer(h, i)
                return 0

            lax.fori_loop(0, 4, one, 0)

        return 0

    lax.fori_loop(0, ticks, tick, 0)

    def tail_hidden(h, _):
        answer_hidden(h)
        return 0

    lax.fori_loop(2, heads, tail_hidden, 0)

    def tail_answer(i, _):
        answer(2 + i % 2, i // 2)
        return 0

    lax.fori_loop(0, 8, tail_answer, 0)

    def arrive(i, _):
        h, k = i // 4, i % 4
        side = early + (k // 2) * (1 - 2 * early)
        block = side * 2 + xx + (k % 2) * (1 - 2 * xx)
        answer_send(h, block).wait_recv()
        mix(frecv[h, :, cols(block)], 1 - y, h, block)
        return 0

    lax.fori_loop(0, heads * 4, arrive, 0)

    def sent_halo(c, _):
        for step in (1, 2):
            @pl.when(halo_here(step, c))
            def _():
                for copy in halo(step, c):
                    copy.wait_send()
        return 0

    lax.fori_loop(0, KV_HEADS, sent_halo, 0)

    @pl.when(is_source)
    def _():
        for k in range(2):
            spare(k).wait_send()

    @pl.when(is_relay)
    def _():
        for k in range(2):
            for i in range(late):
                onward(k, i).wait_send()

    def sent(p, _):
        hs, m = piece(p)
        for k in range(2):
            s0(2 * hs + k, m).wait_send()
        for q in bands:
            xa(p, q).wait_send()
            gax(p, cb, q).wait_send()
            for k in range(2):
                for j in range(2):
                    pair(2 * hs + k, m, j, q).wait_send()

        @pl.when(place < top)
        def _():
            for q in bands:
                za(p, q).wait_send()
                for j in range(2):
                    zb(p, j, q).wait_send()

        @pl.when(place > 0)
        def _():
            for q in bands:
                gaz(p, q).wait_send()
                for j in range(2):
                    gbz(p, j, q).wait_send()

        @pl.when(is_root)
        def _():
            for q in bands:
                xb(p, q).wait_send()
                gbx(p, cb, q).wait_send()

        return 0

    lax.fori_loop(0, pieces, sent, 0)

    def sent_y(i, _):
        answer_send(i // 4, i % 4).wait_send()
        return 0

    lax.fori_loop(0, heads * 4, sent_y, 0)


def fused(fw_query, fw_key, fw_value, learn_rate, fast_weights, attn_query, attn_key, attn_value):
    tokens, heads, width = fw_key.shape[0], fast_weights.shape[1], fast_weights.shape[2]
    rows, kv_width = attn_key.shape
    span = -(-(WINDOW + rows) // LANES) * LANES
    bf, f32 = jnp.bfloat16, jnp.float32
    anywhere = pl.BlockSpec(memory_space=pl.ANY)
    vmem = pl.BlockSpec(memory_space=pltpu.VMEM)
    dma = pltpu.SemaphoreType.DMA
    pieces = heads // 2 * 3
    return pl.pallas_call(
        functools.partial(fused_kernel, heads, width, rows),
        out_shape=pltpu.VMEM(attn_query.shape, bf),
        in_specs=[anywhere, anywhere, anywhere, anywhere, anywhere, anywhere, anywhere, anywhere],
        out_specs=vmem,
        scratch_shapes=[
            pltpu.VMEM(fw_query.shape, bf),
            pltpu.VMEM(fw_key.shape, bf),
            pltpu.VMEM(fw_value.shape, bf),
            pltpu.VMEM(fast_weights.shape, bf),
            pltpu.VMEM(attn_query.shape, bf),
            pltpu.VMEM((span, kv_width), bf),
            pltpu.VMEM((span, kv_width), bf),
            pltpu.VMEM((heads, 3, width, width), bf),
            pltpu.VMEM((heads, 3, width, 2 * LANES), bf),
            pltpu.VMEM((pieces, width, LANES), bf),
            pltpu.VMEM((pieces, width, LANES), bf),
            pltpu.VMEM((pieces, width, LANES), bf),
            pltpu.VMEM((pieces, 2, width, LANES), bf),
            pltpu.VMEM((heads, 3, width, width), bf),
            pltpu.VMEM(attn_query.shape, f32),
            pltpu.VMEM((rows, span), f32),
            pltpu.VMEM((heads, tokens, width), bf),
            pltpu.VMEM((heads, rows, width), bf),
            pltpu.VMEM((heads, rows, width), bf),
            pltpu.VMEM((heads, tokens), f32),
            pltpu.VMEM((heads, tokens, LANES), f32),
            pltpu.VMEM((2, rows, (KV_HEADS - DIRECT) * LANES), bf),
            dma((heads, 3)), dma((5,)), dma((4, KV_HEADS)), dma((4, KV_HEADS)),
            dma((heads, 3)), dma((heads, 3)), *[dma((pieces, SPLIT))] * 6, *[dma((pieces, 2, SPLIT))] * 2,
            *[dma((pieces, SPLIT))] * 6, *[dma((pieces, 2, SPLIT))] * 2,
            *[dma((heads, 3, 2, SPLIT))] * 2, *[dma((heads, 4))] * 2,
            dma((2,)), dma((2,)), dma((2, KV_HEADS - DIRECT)),
        ],
        compiler_params=pltpu.CompilerParams(
            collective_id=0, has_side_effects=True, vmem_limit_bytes=60 * 1024 * 1024
        ),
    )(fw_query, fw_key, fw_value, learn_rate.T, fast_weights, attn_query, attn_key, attn_value)


def takes_fused(mesh, args):
    tokens, rows = args[1].shape[0], args[5].shape[0]
    heads, width = args[4].shape[1], args[4].shape[2]
    return (
        mesh.shape["seq"] == 16
        and mesh.shape["head"] == 2
        and heads == 4
        and width == 4 * LANES
        and tokens == 2 * rows
        and rows < WINDOW < 2 * rows
        and (-(WINDOW + rows)) % LANES > 0
    )


def solution(mesh):
    placed = (
        P("seq", "head"),
        P("seq", "head"),
        P("seq", "head"),
        P("seq", "head"),
        P(None, "head", None, None),
        P(("seq", "head"), None),
        P(("seq", "head"), None),
        P(("seq", "head"), None),
    )

    def body(*args):
        return fused(*args) if takes_fused(mesh, args) else on_device(*args)

    return jax.shard_map(
        body, mesh=mesh, in_specs=placed, out_specs=P(("seq", "head"), None), check_vma=False
    )
```

profile of v0, /device:TPU:0, one launch (start us, length us, event | category | flops | bytes accessed | tf_op | source)
XLA Modules:
  0.0 95.9 jit_solution(11026629029773460372)
XLA Ops:
  0.0 94.8 %shard_map.82 = bf16[192,4096]{1,0:T(8,128)(2,1)S(1)} custom-call(bf16[384,2048]{1,0:T(8,128)(2,1)} %q_hbm.1, bf16[384,2048]{1,0:T(8,128)(2,1)} %k_hbm.1, bf16[384,2048]{1,0:T(8,128)(2,1)} %v_hbm.1, f32[4,384]{1,0:T(4,128)} %bitcast.1, bf16[3,4,512,512]{3,2,1,0:T(8,128)(2,1)} %w_hbm.1, bf16[192,4096]{1,0:T(8,128)(2,1)} %aq_hbm.1, bf16[192,1024]{1,0:T(8,128)(2,1)} %ak_hbm.1, ...), custom_call_target="tpu_custom_call" | custom-call | tf_op jit(solution)/shard_map/pallas_call | solution.py:776
  94.8 1.1 %copy.10 = bf16[192,4096]{1,0:T(8,128)(2,1)} copy(bf16[192,4096]{1,0:T(8,128)(2,1)S(1)} %shard_map.82) | data formatting | bytes 3145728
where the time goes:
time: 96.8 us; the launch traced here: 95.9 us
  Pallas kernels  94.8 us (98%)
  local copies, waits for them, and re-layouts  1.15 us (1%)
    pallas_call x1, Pallas kernels, fused(): pl.pallas_call(functools.partial(fused_kernel, heads, width, rows), out_s...  94.8 us

commit v1 on v0

--- a/solution.py
+++ b/solution.py
@@ -108,14 +108,20 @@
 
 MESH = pl.DeviceIdType.MESH
 LANES = 128
+A_FIRST = 0
+DOWN_A_FIRST = 0
+LAST_EARLY = 0
 SPLIT = 1
-LAG_A = 2
-ROOT_B = 5
-ROOT_A = 5
+LAG_A = 3
+ROOT_B = 6
+ROOT_A = 6
 FIRST_ATT = 4
 PREPARE = 2
-DIRECT = 4
-RELAY_AT = 1
+RELAY_AT = 2
+NEAR_AT = -1
+FAR_AT = -1
+ATT_SPLIT = 0
+B_AHEAD = 0
 
 
 def piece(p):
@@ -214,73 +220,65 @@
         def _():
             greet((pos - step) // n_head, (pos - step) % n_head)
 
-    def halo(step, c):
-        there = pos + step
-        seq, head = there // n_head, there % n_head
-        if step == 1:
-            src, dst = pl.ds(0, rows), pl.ds(pad + extra, rows)
-        else:
-            src, dst = pl.ds(rows - extra, extra), pl.ds(pad, extra)
-        j = (step - 1) * 2
-        return (
-            remote(ak_hbm.at[src, cols(c)], akb.at[dst, cols(c)], halo_s.at[j, c], halo_r.at[j, c], seq, head),
-            remote(av_hbm.at[src, cols(c)], avb.at[dst, cols(c)], halo_s.at[j + 1, c], halo_r.at[j + 1, c], seq, head),
-        )
-
-    across = core * y
-    late = KV_HEADS - DIRECT
-    late_cols = pl.ds(DIRECT * LANES, late * LANES)
+    def place_of(step):
+        return (pos + step) // n_head, (pos + step) % n_head
+
+    wide = KV_HEADS // 2 * LANES
+    near_at, far_at = pl.ds(pad + extra, rows), pl.ds(pad, extra)
+
+    def near_rows(b):
+        return [
+            remote(hbm.at[:, cols(b, wide)], ref.at[near_at, cols(b, wide)], halo_s.at[k, b], halo_r.at[k, b], *place_of(1))
+            for k, (hbm, ref) in enumerate(((ak_hbm, akb), (av_hbm, avb)))
+        ]
+
+    def far_rows():
+        return [
+            remote(hbm.at[pl.ds(rows - extra, extra)], ref.at[far_at], halo_s.at[k, 2], halo_r.at[k, 2], *place_of(2))
+            for k, (hbm, ref) in enumerate(((ak_hbm, akb), (av_hbm, avb)))
+        ]
 
     def spare(k):
         hbm = (ak_hbm, av_hbm)[k]
-        return remote(hbm.at[:, late_cols], via.at[k], via_s.at[k], via_r.at[k], me, 1 - y)
-
-    def onward(k, i):
+        return remote(hbm.at[:, cols(1, wide)], via.at[k], via_s.at[k], via_r.at[k], me, 1 - y)
+
+    def onward(k):
         ref = (akb, avb)[k]
-        at = cols(DIRECT + i)
-        return remote(
-            via.at[k, :, cols(i)], ref.at[pl.ds(pad + extra, rows), at],
-            on_s.at[k, i], halo_r.at[k, DIRECT + i], (pos + 2) // n_head, (pos + 2) % n_head,
-        )
-
+        return remote(via.at[k], ref.at[near_at, cols(1, wide)], on_s.at[k], halo_r.at[k, 1], *place_of(2))
+
+    across = core * y
     is_source = (across == 1) & (pos + 1 < last)
     is_relay = (core == 1) & (y == 0) & (pos + 2 < last)
 
-    def halo_here(step, c):
-        if step == 2:
-            return pos + 2 < last
-        return (pos + 1 < last) & ((c < DIRECT) | (across == 0))
-
-    def halo_start(c, _):
-        @pl.when(halo_here(1, c))
-        def _():
-            for copy in halo(1, c):
+    def near_first():
+        @pl.when(pos + 1 < last)
+        def _():
+            for copy in near_rows(0):
                 copy.start()
 
-        return 0
-
-    def halo_start_far(c, _):
-        @pl.when(halo_here(2, c))
-        def _():
-            for copy in halo(2, c):
-                copy.start()
-
-        return 0
-
-    def relay_start():
         @pl.when(is_source)
         def _():
             for k in range(2):
                 spare(k).start()
 
+    def near_second():
+        @pl.when((pos + 1 < last) & (across == 0))
+        def _():
+            for copy in near_rows(1):
+                copy.start()
+
+    def far_start():
+        @pl.when(pos + 2 < last)
+        def _():
+            for copy in far_rows():
+                copy.start()
+
     def relay_on():
         @pl.when(is_relay)
         def _():
             for k in range(2):
                 spare(k).wait_recv()
-            for i in range(late):
-                for k in range(2):
-                    onward(k, i).start()
+                onward(k).start()
 
     depth = width // SPLIT
     bands = range(SPLIT)
@@ -394,18 +392,21 @@
     def own_whole(h, m):
         return f32(g[h, m, :, cols(cb)]) + f32(r0[h, m, :, cols(xx)])
 
-    def stage_in(p):
-        hs, m = piece(p)
-        h = 2 * hs
-        s0(h + 1, m).wait_recv()
+    def stage_in_b(p):
+        hs, m = piece(p)
+        h = 2 * hs + 1
+        s0(h, m).wait_recv()
 
         @pl.when(place == 0)
         def _():
             for j in range(2):
                 for q in bands:
-                    keep_sum(h + 1, m, core * 2 + j, q, own(h + 1, m, core * 2 + j, j, q))
+                    keep_sum(h, m, core * 2 + j, q, own(h, m, core * 2 + j, j, q))
                     zb(p, j, q).start()
 
+    def stage_in_a(p):
+        hs, m = piece(p)
+        h = 2 * hs
         s0(h, m).wait_recv()
         for q in bands:
             keep_sum(h, m, ob, q, own(h, m, ob, 1 - xx, q))
@@ -527,16 +528,21 @@
     group = Q_HEADS // KV_HEADS
     scaling = 1.0 / math.sqrt(HEAD_DIM)
 
-    def attend(c):
-        for step in (1, 2):
-            @pl.when(pos >= step)
-            def _():
-                for copy in halo(step, c):
-                    copy.wait_recv()
-
+    def neighbours_here(c):
+        @pl.when((c % (KV_HEADS // 2) == 0) & (pos >= 1))
+        def _():
+            for copy in near_rows(c // (KV_HEADS // 2)):
+                copy.wait_recv()
+
+        @pl.when((c == 0) & (pos >= 2))
+        def _():
+            for copy in far_rows():
+                copy.wait_recv()
+
+    def attend(c, heads_of):
         keys = akb[:, cols(c)]
         vals = avb[:, cols(c)]
-        for j in range(group):
+        for j in heads_of:
             qc = cols(c * group + j)
             scores = lax.dot_general(
                 aqb[:, qc], keys, (((1,), (1,)), ((), ())), preferred_element_type=jnp.float32
@@ -547,6 +553,15 @@
             probs = (expo / jnp.sum(expo, axis=-1, keepdims=True)).astype(jnp.bfloat16)
             att[:, qc] = jnp.dot(probs, vals, preferred_element_type=jnp.float32)
 
+    def attend_part(t, heads_of):
+        c = t - FIRST_ATT
+
+        @pl.when((c >= 0) & (c < KV_HEADS))
+        def _():
+            if heads_of[0] == 0:
+                neighbours_here(c)
+            attend(c, heads_of)
+
     def answer_send(h, block):
         return remote(
             fsend.at[h, :, cols(block)], frecv.at[h, :, cols(block)], y_s.at[h, block], y_r.at[h, block], me, 1 - y
@@ -600,9 +615,11 @@
     pl.semaphore_wait(barrier, met)
     for m in range(3):
         s0(1, m).start()
-    relay_start()
-    lax.fori_loop(0, KV_HEADS, halo_start, 0)
-    lax.fori_loop(0, KV_HEADS, halo_start_far, 0)
+    for at, go in ((NEAR_AT, near_first), (FAR_AT, far_start), (NEAR_AT, near_second)):
+        if at < 0:
+            go()
+    if B_AHEAD:
+        stage_in_b(0)
     compute(0)
 
     def prepare():
@@ -627,15 +644,19 @@
     ticks = pieces + max(ROOT_A, ROOT_B) + (n_seq // 4 - 1) + 1
 
     def tick(t, _):
-        during(t, stage_in)
+        during(t + B_AHEAD, stage_in_b)
+        during(t, stage_in_a)
 
         @pl.when(t < heads - 2)
         def _():
             compute(heads - 1 - t)
 
-        @pl.when(t == RELAY_AT)
-        def _():
-            relay_on()
+        for at, go in ((NEAR_AT, near_first), (FAR_AT, far_start), (NEAR_AT, near_second), (RELAY_AT, relay_on)):
+            if at >= 0:
+                @pl.when(t == at)
+                def _():
+                    go()
+
 
         @pl.when(place > 0)
         def _():
@@ -643,26 +664,35 @@
 
         during(t - LAG_A - place, stage_a)
 
+        if ATT_SPLIT:
+            attend_part(t, range(ATT_SPLIT))
+
         @pl.when(is_root)
         def _():
-            during(t - ROOT_B, stage_root_b)
-            during(t - ROOT_A, stage_root_a)
+            for at, stage in ((ROOT_A, stage_root_a), (ROOT_B, stage_root_b))[:: 1 if A_FIRST else -1]:
+                during(t - at, stage)
 
         @pl.when(place < top)
         def _():
-            during(t - ROOT_A - top + place, stage_down_a)
-            during(t - ROOT_B - top + place, stage_down_b)
-
+            for at, stage in ((ROOT_A, stage_down_a), (ROOT_B, stage_down_b))[:: 1 if DOWN_A_FIRST else -1]:
+                during(t - at - top + place, stage)
+
+        @pl.when(t == ticks - 1)
+        def _():
+            for h in range(2, heads):
+                answer_hidden(h)
+
+        if LAST_EARLY:
+            during(t - ROOT_A - 1 - top + place, stage_last_a)
         during(t - ROOT_B - 1 - top + place, stage_last_b)
-        during(t - ROOT_A - 1 - top + place, stage_last_a)
+        if not LAST_EARLY:
+            during(t - ROOT_A - 1 - top + place, stage_last_a)
 
         @pl.when(t == PREPARE)
         def _():
             prepare()
 
-        @pl.when((t >= FIRST_ATT) & (t < FIRST_ATT + KV_HEADS))
-        def _():
-            attend(t - FIRST_ATT)
+        attend_part(t, range(ATT_SPLIT, group))
 
         @pl.when((t >= done) & (t < done + 2))
         def _():
@@ -679,17 +709,70 @@
 
     lax.fori_loop(0, ticks, tick, 0)
 
-    def tail_hidden(h, _):
-        answer_hidden(h)
-        return 0
-
-    lax.fori_loop(2, heads, tail_hidden, 0)
-
     def tail_answer(i, _):
         answer(2 + i % 2, i // 2)
         return 0
 
     lax.fori_loop(0, 8, tail_answer, 0)
+
+    @pl.when(pos + 1 < last)
+    def _():
+        for copy in near_rows(0):
+            copy.wait_send()
+
+    @pl.when((pos + 1 < last) & (across == 0))
+    def _():
+        for copy in near_rows(1):
+            copy.wait_send()
+
+    @pl.when(pos + 2 < last)
+    def _():
+        for copy in far_rows():
+            copy.wait_send()
+
+    for k in range(2):
+        @pl.when(is_source)
+        def _():
+            spare(k).wait_send()
+
+        @pl.when(is_relay)
+        def _():
+            onward(k).wait_send()
+
+    def sent(p, _):
+        hs, m = piece(p)
+        for k in range(2):
+            s0(2 * hs + k, m).wait_send()
+        for q in bands:
+            xa(p, q).wait_send()
+            gax(p, cb, q).wait_send()
+            for k in range(2):
+                for j in range(2):
+                    pair(2 * hs + k, m, j, q).wait_send()
+
+        @pl.when(place < top)
+        def _():
+            for q in bands:
+                za(p, q).wait_send()
+                for j in range(2):
+                    zb(p, j, q).wait_send()
+
+        @pl.when(place > 0)
+        def _():
+            for q in bands:
+                gaz(p, q).wait_send()
+                for j in range(2):
+                    gbz(p, j, q).wait_send()
+
+        @pl.when(is_root)
+        def _():
+            for q in bands:
+                xb(p, q).wait_send()
+                gbx(p, cb, q).wait_send()
+
+        return 0
+
+    lax.fori_loop(0, pieces, sent, 0)
 
     def arrive(i, _):
         h, k = i // 4, i % 4
@@ -700,62 +783,6 @@
         return 0
 
     lax.fori_loop(0, heads * 4, arrive, 0)
-
-    def sent_halo(c, _):
-        for step in (1, 2):
-            @pl.when(halo_here(step, c))
-            def _():
-                for copy in halo(step, c):
-                    copy.wait_send()
-        return 0
-
-    lax.fori_loop(0, KV_HEADS, sent_halo, 0)
-
-    @pl.when(is_source)
-    def _():
-        for k in range(2):
-            spare(k).wait_send()
-
-    @pl.when(is_relay)
-    def _():
-        for k in range(2):
-            for i in range(late):
-                onward(k, i).wait_send()
-
-    def sent(p, _):
-        hs, m = piece(p)
-        for k in range(2):
-            s0(2 * hs + k, m).wait_send()
-        for q in bands:
-            xa(p, q).wait_send()
-            gax(p, cb, q).wait_send()
-            for k in range(2):
-                for j in range(2):
-                    pair(2 * hs + k, m, j, q).wait_send()
-
-        @pl.when(place < top)
-        def _():
-            for q in bands:
-                za(p, q).wait_send()
-                for j in range(2):
-                    zb(p, j, q).wait_send()
-
-        @pl.when(place > 0)
-        def _():
-            for q in bands:
-                gaz(p, q).wait_send()
-                for j in range(2):
-                    gbz(p, j, q).wait_send()
-
-        @pl.when(is_root)
-        def _():
-            for q in bands:
-                xb(p, q).wait_send()
-                gbx(p, cb, q).wait_send()
-
-        return 0
-
-    lax.fori_loop(0, pieces, sent, 0)
 
     def sent_y(i, _):
         answer_send(i // 4, i % 4).wait_send()
@@ -800,12 +827,12 @@
             pltpu.VMEM((heads, rows, width), bf),
             pltpu.VMEM((heads, tokens), f32),
             pltpu.VMEM((heads, tokens, LANES), f32),
-            pltpu.VMEM((2, rows, (KV_HEADS - DIRECT) * LANES), bf),
-            dma((heads, 3)), dma((5,)), dma((4, KV_HEADS)), dma((4, KV_HEADS)),
+            pltpu.VMEM((2, rows, kv_width // 2), bf),
+            dma((heads, 3)), dma((5,)), dma((2, 3)), dma((2, 3)),
             dma((heads, 3)), dma((heads, 3)), *[dma((pieces, SPLIT))] * 6, *[dma((pieces, 2, SPLIT))] * 2,
             *[dma((pieces, SPLIT))] * 6, *[dma((pieces, 2, SPLIT))] * 2,
             *[dma((heads, 3, 2, SPLIT))] * 2, *[dma((heads, 4))] * 2,
-            dma((2,)), dma((2,)), dma((2, KV_HEADS - DIRECT)),
+            dma((2,)), dma((2,)), dma((2,)),
         ],
         compiler_params=pltpu.CompilerParams(
             collective_id=0, has_side_effects=True, vmem_limit_bytes=60 * 1024 * 1024

time: 96.8 us -> 91.9 us (0.949)
  Pallas kernels: 94.8 us -> 90.6 us
    pallas_call x1, Pallas kernels: 94.8 us -> 90.6 us  [fused(): pl.pallas_call(functools.partial(fused_kernel, heads, width, rows), out_s...]
where the time goes in v1:
time: 91.9 us; the launch traced here: 91.8 us
  Pallas kernels  90.6 us (99%)
  local copies, waits for them, and re-layouts  1.15 us (1%)
    pallas_call x1, Pallas kernels, fused(): pl.pallas_call(functools.partial(fused_kernel, heads, width, rows), out_s...  90.6 us

profile of v1, /device:TPU:0, one launch (start us, length us, event | category | flops | bytes accessed | tf_op | source)
XLA Modules:
  0.0 91.8 jit_solution(3904994065620717484)
XLA Ops:
  0.0 90.6 %shard_map.82 = bf16[192,4096]{1,0:T(8,128)(2,1)S(1)} custom-call(bf16[384,2048]{1,0:T(8,128)(2,1)} %q_hbm.1, bf16[384,2048]{1,0:T(8,128)(2,1)} %k_hbm.1, bf16[384,2048]{1,0:T(8,128)(2,1)} %v_hbm.1, f32[4,384]{1,0:T(4,128)} %bitcast.1, bf16[3,4,512,512]{3,2,1,0:T(8,128)(2,1)} %w_hbm.1, bf16[192,4096]{1,0:T(8,128)(2,1)} %aq_hbm.1, bf16[192,1024]{1,0:T(8,128)(2,1)} %ak_hbm.1, ...), custom_call_target="tpu_custom_call" | custom-call | tf_op jit(solution)/shard_map/pallas_call | solution.py:803
  90.6 1.1 %copy.10 = bf16[192,4096]{1,0:T(8,128)(2,1)} copy(bf16[192,4096]{1,0:T(8,128)(2,1)S(1)} %shard_map.82) | data formatting | bytes 3145728

commit v2 on v1

--- a/solution.py
+++ b/solution.py
@@ -108,6 +108,7 @@
 
 MESH = pl.DeviceIdType.MESH
 LANES = 128
+TURN = 1
 A_FIRST = 0
 DOWN_A_FIRST = 0
 LAST_EARLY = 0
@@ -140,13 +141,13 @@
     n_seq, n_head = lax.axis_size("seq"), lax.axis_size("head")
     core, xx, z = me % 2, (me // 2) % 2, me // 4
     top = n_seq // 4 - 1
-    place = z + core * (top - 2 * z)
+    place = z + ((1 - TURN) // 2 + core * TURN) * (top - 2 * z)
     cb = core * 2 + xx
     ob = core * 2 + 1 - xx
     other_core = me + 1 - 2 * core
     other_x = me + 2 - 4 * xx
-    ahead = me + 4 - 8 * core
-    behind = me - 4 + 8 * core
+    ahead = (me + n_seq + (4 - 8 * core) * TURN) % n_seq
+    behind = (me + n_seq - (4 - 8 * core) * TURN) % n_seq
     pos = me * n_head + y
     last = n_seq * n_head
     extra = WINDOW - rows
@@ -221,7 +222,8 @@
             greet((pos - step) // n_head, (pos - step) % n_head)
 
     def place_of(step):
-        return (pos + step) // n_head, (pos + step) % n_head
+        there = (pos + step) % last
+        return there // n_head, there % n_head
 
     wide = KV_HEADS // 2 * LANES
     near_at, far_at = pl.ds(pad + extra, rows), pl.ds(pad, extra)

time: 91.9 us -> 91.9 us (level)
  no operation moved by 1% of the time
where the time goes in v2:
time: 91.9 us; the launch traced here: 91.8 us
  Pallas kernels  90.6 us (99%)
  local copies, waits for them, and re-layouts  1.15 us (1%)
    pallas_call x1, Pallas kernels, fused(): pl.pallas_call(functools.partial(fused_kernel, heads, width, rows), out_s...  90.6 us

profile of v2, /device:TPU:0, one launch (start us, length us, event | category | flops | bytes accessed | tf_op | source)
XLA Modules:
  0.0 91.8 jit_solution(3378875208090632646)
XLA Ops:
  0.0 90.6 %shard_map.82 = bf16[192,4096]{1,0:T(8,128)(2,1)S(1)} custom-call(bf16[384,2048]{1,0:T(8,128)(2,1)} %q_hbm.1, bf16[384,2048]{1,0:T(8,128)(2,1)} %k_hbm.1, bf16[384,2048]{1,0:T(8,128)(2,1)} %v_hbm.1, f32[4,384]{1,0:T(4,128)} %bitcast.1, bf16[3,4,512,512]{3,2,1,0:T(8,128)(2,1)} %w_hbm.1, bf16[192,4096]{1,0:T(8,128)(2,1)} %aq_hbm.1, bf16[192,1024]{1,0:T(8,128)(2,1)} %ak_hbm.1, ...), custom_call_target="tpu_custom_call" | custom-call | tf_op jit(solution)/shard_map/pallas_call | solution.py:805
  90.6 1.1 %copy.10 = bf16[192,4096]{1,0:T(8,128)(2,1)} copy(bf16[192,4096]{1,0:T(8,128)(2,1)S(1)} %shard_map.82) | data formatting | bytes 3145728

commit v3 on v2

--- a/solution.py
+++ b/solution.py
@@ -116,13 +116,15 @@
 LAG_A = 3
 ROOT_B = 6
 ROOT_A = 6
-FIRST_ATT = 4
+FIRST_ATT = 5
 PREPARE = 2
 RELAY_AT = 2
 NEAR_AT = -1
 FAR_AT = -1
 ATT_SPLIT = 0
 B_AHEAD = 0
+NEAR = 4
+PASS_EARLY = 1
 
 
 def piece(p):
@@ -134,7 +136,7 @@
     q_hbm, k_hbm, v_hbm, rate_hbm, w_hbm, aq_hbm, ak_hbm, av_hbm, out_ref,
     qb, kb, vb, wb, aqb, akb, avb, g, r0, rxa, rza, rxb, rzb, nw, att, bias, hidb, fsend, frecv, rate_ref, rates, via,
     in_sem, misc_sem, halo_s, halo_r, s0_s, s0_r, xa_s, xa_r, za_s, za_r, xb_s, xb_r, zb_s, zb_r,
-    gax_s, gax_r, gaz_s, gaz_r, gbx_s, gbx_r, gbz_s, gbz_r, c_s, c_r, y_s, y_r, via_s, via_r, on_s,
+    gax_s, gax_r, gaz_s, gaz_r, gbx_s, gbx_r, gbz_s, gbz_r, c_s, c_r, y_s, y_r, via_s, via_r, on_s, pass_s,
 ):
     me = lax.axis_index("seq")
     y = lax.axis_index("head")
@@ -225,28 +227,44 @@
         there = (pos + step) % last
         return there // n_head, there % n_head
 
-    wide = KV_HEADS // 2 * LANES
+    def part(b):
+        return pl.ds(b * NEAR * LANES, (b * KV_HEADS + (1 - 2 * b) * NEAR) * LANES)
+
     near_at, far_at = pl.ds(pad + extra, rows), pl.ds(pad, extra)
 
     def near_rows(b):
         return [
-            remote(hbm.at[:, cols(b, wide)], ref.at[near_at, cols(b, wide)], halo_s.at[k, b], halo_r.at[k, b], *place_of(1))
+            remote(hbm.at[:, part(b)], ref.at[near_at, part(b)], halo_s.at[k, b], halo_r.at[k, b], *place_of(1))
             for k, (hbm, ref) in enumerate(((ak_hbm, akb), (av_hbm, avb)))
         ]
 
-    def far_rows():
+    def far_rows(b):
         return [
-            remote(hbm.at[pl.ds(rows - extra, extra)], ref.at[far_at], halo_s.at[k, 2], halo_r.at[k, 2], *place_of(2))
+            remote(
+                hbm.at[pl.ds(rows - extra, extra), part(b)], ref.at[far_at, part(b)],
+                halo_s.at[k, 2 + b], halo_r.at[k, 2 + b], *place_of(2),
+            )
             for k, (hbm, ref) in enumerate(((ak_hbm, akb), (av_hbm, avb)))
         ]
 
+    def pass_rows(b):
+        return [
+            remote(
+                ref.at[pl.ds(pad + rows, extra), part(b)], ref.at[far_at, part(b)],
+                pass_s.at[k, b], halo_r.at[k, 2 + b], me, 1 - y,
+            )
+            for k, ref in enumerate((akb, avb))
+        ]
+
+    passes = (core == 0) & (y == 0) & (me > 0)
+
     def spare(k):
         hbm = (ak_hbm, av_hbm)[k]
-        return remote(hbm.at[:, cols(1, wide)], via.at[k], via_s.at[k], via_r.at[k], me, 1 - y)
+        return remote(hbm.at[:, part(1)], via.at[k], via_s.at[k], via_r.at[k], me, 1 - y)
 
     def onward(k):
         ref = (akb, avb)[k]
-        return remote(via.at[k], ref.at[near_at, cols(1, wide)], on_s.at[k], halo_r.at[k, 1], *place_of(2))
+        return remote(via.at[k], ref.at[near_at, part(1)], on_s.at[k], halo_r.at[k, 1], *place_of(2))
 
     across = core * y
     is_source = (across == 1) & (pos + 1 < last)
@@ -270,10 +288,11 @@
                 copy.start()
 
     def far_start():
-        @pl.when(pos + 2 < last)
-        def _():
-            for copy in far_rows():
-                copy.start()
+        @pl.when((pos + 2 < last) & (across == 0))
+        def _():
+            for b in range(2):
+                for copy in far_rows(b):
+                    copy.start()
 
     def relay_on():
         @pl.when(is_relay)
@@ -530,15 +549,21 @@
     group = Q_HEADS // KV_HEADS
     scaling = 1.0 / math.sqrt(HEAD_DIM)
 
-    def neighbours_here(c):
-        @pl.when((c % (KV_HEADS // 2) == 0) & (pos >= 1))
-        def _():
-            for copy in near_rows(c // (KV_HEADS // 2)):
+    def near_here(b):
+        @pl.when(pos >= 1)
+        def _():
+            for copy in near_rows(b):
                 copy.wait_recv()
 
-        @pl.when((c == 0) & (pos >= 2))
-        def _():
-            for copy in far_rows():
+        @pl.when(passes)
+        def _():
+            for copy in pass_rows(b):
+                copy.start()
+
+    def far_here(b):
+        @pl.when(pos >= 2)
+        def _():
+            for copy in far_rows(b):
                 copy.wait_recv()
 
     def attend(c, heads_of):
@@ -552,7 +577,7 @@
             scores = jnp.where(bias[...] > 0.0, scores, -1e30)
             peak = jnp.max(scores, axis=-1, keepdims=True)
             expo = jnp.exp(scores - peak)
-            probs = (expo / jnp.sum(expo, axis=-1, keepdims=True)).astype(jnp.bfloat16)
+            probs = (expo * (1.0 / jnp.sum(expo, axis=-1, keepdims=True))).astype(jnp.bfloat16)
             att[:, qc] = jnp.dot(probs, vals, preferred_element_type=jnp.float32)
 
     def attend_part(t, heads_of):
@@ -560,8 +585,11 @@
 
         @pl.when((c >= 0) & (c < KV_HEADS))
         def _():
-            if heads_of[0] == 0:
-                neighbours_here(c)
+            for b in range(2):
+                @pl.when(c == b * NEAR)
+                def _():
+                    far_here(b)
+
             attend(c, heads_of)
 
     def answer_send(h, block):
@@ -696,6 +724,12 @@
 
         attend_part(t, range(ATT_SPLIT, group))
 
+        for b in range(2):
+            @pl.when(t == FIRST_ATT - 1 - PASS_EARLY + b * NEAR)
+            def _():
+                near_here(b)
+
+
         @pl.when((t >= done) & (t < done + 2))
         def _():
             h = t - done
@@ -727,10 +761,17 @@
         for copy in near_rows(1):
             copy.wait_send()
 
-    @pl.when(pos + 2 < last)
+    @pl.when((pos + 2 < last) & (across == 0))
     def _():
-        for copy in far_rows():
-            copy.wait_send()
+        for b in range(2):
+            for copy in far_rows(b):
+                copy.wait_send()
+
+    @pl.when(passes)
+    def _():
+        for b in range(2):
+            for copy in pass_rows(b):
+                copy.wait_send()
 
     for k in range(2):
         @pl.when(is_source)
@@ -829,12 +870,12 @@
             pltpu.VMEM((heads, rows, width), bf),
             pltpu.VMEM((heads, tokens), f32),
             pltpu.VMEM((heads, tokens, LANES), f32),
-            pltpu.VMEM((2, rows, kv_width // 2), bf),
-            dma((heads, 3)), dma((5,)), dma((2, 3)), dma((2, 3)),
+            pltpu.VMEM((2, rows, (KV_HEADS - NEAR) * LANES), bf),
+            dma((heads, 3)), dma((5,)), dma((2, 4)), dma((2, 4)),
             dma((heads, 3)), dma((heads, 3)), *[dma((pieces, SPLIT))] * 6, *[dma((pieces, 2, SPLIT))] * 2,
             *[dma((pieces, SPLIT))] * 6, *[dma((pieces, 2, SPLIT))] * 2,
             *[dma((heads, 3, 2, SPLIT))] * 2, *[dma((heads, 4))] * 2,
-            dma((2,)), dma((2,)), dma((2,)),
+            dma((2,)), dma((2,)), dma((2,)), dma((2, 2)),
         ],
         compiler_params=pltpu.CompilerParams(
             collective_id=0, has_side_effects=True, vmem_limit_bytes=60 * 1024 * 1024

time: 91.9 us -> 91.6 us (level)
  no operation moved by 1% of the time
where the time goes in v3:
time: 91.6 us; the launch traced here: 91.4 us
  Pallas kernels  90.3 us (99%)
  local copies, waits for them, and re-layouts  1.15 us (1%)
    pallas_call x1, Pallas kernels, fused(): pl.pallas_call(functools.partial(fused_kernel, heads, width, rows), out_s...  90.3 us

profile of v3, /device:TPU:0, one launch (start us, length us, event | category | flops | bytes accessed | tf_op | source)
XLA Modules:
  0.0 91.4 jit_solution(8021704122200435519)
XLA Ops:
  0.0 90.3 %shard_map.82 = bf16[192,4096]{1,0:T(8,128)(2,1)S(1)} custom-call(bf16[384,2048]{1,0:T(8,128)(2,1)} %q_hbm.1, bf16[384,2048]{1,0:T(8,128)(2,1)} %k_hbm.1, bf16[384,2048]{1,0:T(8,128)(2,1)} %v_hbm.1, f32[4,384]{1,0:T(4,128)} %bitcast.1, bf16[3,4,512,512]{3,2,1,0:T(8,128)(2,1)} %w_hbm.1, bf16[192,4096]{1,0:T(8,128)(2,1)} %aq_hbm.1, bf16[192,1024]{1,0:T(8,128)(2,1)} %ak_hbm.1, ...), custom_call_target="tpu_custom_call" | custom-call | tf_op jit(solution)/shard_map/pallas_call | solution.py:846
  90.3 1.1 %copy.10 = bf16[192,4096]{1,0:T(8,128)(2,1)} copy(bf16[192,4096]{1,0:T(8,128)(2,1)S(1)} %shard_map.82) | data formatting | bytes 3145728
